TPU v7x, 256 devices: a whole 4x4x8 slice. The times are simulated.
256 devices in a mesh: filt: 32 (over y, z_hi, core), space: 8 (over z_lo, x).
Axes of the slice: x: 4, y: 4, z: 8 (z_hi: 4, z_lo: 2; z = z_hi * 2 + z_lo), core: 2. Of those that a mesh axis runs over, the one named last changes fastest.
Arguments:
- volume: bfloat16 [256, 32, 4, 128], P('filt', 'space'), may hold values from -6 to 6
- kernel: bfloat16 [512, 3, 3, 3, 256], P('filt'), may hold values from -0.078125 to 0.078125
- filter_bias: bfloat16 [512], P('filt'), may hold values from -3 to 3
Outputs:
- pooled: bfloat16 [512, 16, 2, 64], P('filt', 'space')
All inputs are finite; a program needn't handle non-finite values.
Results may differ from a plain program's by a relative error of at most 0.001.
Values may be sent and summed in bfloat16 or wider, within the bound.
A program may use at most 64 MiB of HBM per device.

v0:
```python
import jax
import jax.numpy as jnp
from jax import lax
from jax.sharding import PartitionSpec as P

slope = 0.3


def with_halo(block, sides, width):
    for axis, dim in sides:
        count = lax.axis_size(axis)
        forward = [(i, i + 1) for i in range(count - 1)]
        backward = [(target, source) for source, target in forward]
        low = lax.ppermute(
            lax.slice_in_dim(block, block.shape[dim] - width, None, axis=dim), axis, forward
        )
        high = lax.ppermute(lax.slice_in_dim(block, 0, width, axis=dim), axis, backward)
        block = jnp.concatenate([low, block, high], axis=dim)
    return block


def convolve(inputs, weights, padding):
    return lax.conv_general_dilated(
        inputs[None],
        weights,
        (1, 1, 1),
        padding,
        dimension_numbers=("NCDHW", "ODHWI", "NCDHW"),
        preferred_element_type=jnp.float32,
    )[0]


def finish(summed, filter_bias):
    activated = summed + filter_bias.astype(jnp.float32)[:, None, None, None]
    activated = jnp.where(activated > 0, activated, slope * activated)
    filters, depth, height, across = activated.shape
    blocked = activated.reshape(filters, depth // 2, 2, height // 2, 2, across // 2, 2)
    return jnp.max(blocked, axis=(2, 4, 6)).astype(jnp.bfloat16)


def on_device(volume, kernel, filter_bias):
    local_in, slab_depth, height, across = volume.shape
    padded = with_halo(volume, (("space", 1),), 1)
    zeroed = jnp.zeros((kernel.shape[0], slab_depth, height, across), jnp.float32)
    summed = zeroed + convolve(
        lax.all_gather(padded, "filt", axis=0, tiled=True), kernel, ((0, 0), (1, 1), (1, 1))
    )
    return finish(summed, filter_bias)


def solution(mesh):
    in_specs = (P("filt", "space", None, None), P("filt", None, None, None, None), P("filt"))
    out_specs = P("filt", "space", None, None)
    return jax.shard_map(
        on_device, mesh=mesh, in_specs=in_specs, out_specs=out_specs, check_vma=False
    )
```

profile of v0, /device:TPU:1, one launch (start us, length us, event | category | flops | bytes accessed | tf_op | source)
XLA Modules:
  0.0 99.7 jit_solution(1009742245548532842)
XLA Ops:
  6.5 0.0 copy-start
  6.5 0.0 all-gather.2.cloned.1.call-start
  6.5 0.8 fusion.16
  7.3 3.9 %collective-permute-start = (bf16[8,1,4,128]{3,2,1,0:T(4,128)(2,1)S(1)}, bf16[8,1,4,128]{3,2,1,0:T(4,128)(2,1)S(1)}, u32[]{:S(2)}, u32[]{:S(2)}) collective-permute-start(bf16[8,1,4,128]{3,2,1,0:T(4,128)(2,1)S(1)} %get-tuple-element.5), channel_id=1, source_target_pairs={{0,1},{1,2},{2,3},{3,4},{4,5},{5,6},{6,7},{8,9},{9,10},{10,11},{11... | collective-permute-start | bytes 24584 | tf_op jit(solution)/shard_map/ppermute | solution.py:14
  11.2 1.3 %collective-permute-start.1 = (bf16[8,1,4,128]{3,2,1,0:T(4,128)(2,1)S(1)}, bf16[8,1,4,128]{3,2,1,0:T(4,128)(2,1)S(1)}, u32[]{:S(2)}, u32[]{:S(2)}) collective-permute-start(bf16[8,1,4,128]{3,2,1,0:T(4,128)(2,1)S(1)} %get-tuple-element.6), channel_id=1, source_target_pairs={{1,0},{2,1},{3,2},{4,3},{5,4},{6,5},{7,6},{9,8},{10,9},{11,10},{12... | collective-permute-start | bytes 24584 | tf_op jit(solution)/shard_map/ppermute | solution.py:17
  12.5 0.0 collective-permute-done
  12.6 3.1 %collective-permute-done.1 = bf16[8,1,4,128]{3,2,1,0:T(4,128)(2,1)S(1)} collective-permute-done((bf16[8,1,4,128]{3,2,1,0:T(4,128)(2,1)S(1)}, bf16[8,1,4,128]{3,2,1,0:T(4,128)(2,1)S(1)}, u32[]{:S(2)}, u32[]{:S(2)}) %collective-permute-start.1) | collective-permute-done | bytes 8224 | tf_op jit(solution)/shard_map/ppermute | solution.py:17
  15.6 1.4 %pad_maximum_fusion = bf16[8,6,4,128]{3,2,1,0:T(4,128)(2,1)} fusion(bf16[8,1,4,128]{3,2,1,0:T(4,128)(2,1)S(1)} %collective-permute-done.1, bf16[8,4,4,128]{3,2,1,0:T(4,128)(2,1)} %param.3, bf16[8,1,4,128]{3,2,1,0:T(4,128)(2,1)S(1)} %collective-permute-done), kind=kLoop, calls=%fused_computation.13 | loop fusion | flops 49152 | bytes 98304 | tf_op jit(solution)/shard_map/concatenate | solution.py:18
  17.1 0.0 all-gather.2.cloned.1.call-update
  17.1 0.7 convert_element_type.6
  17.7 58.8 %all-gather.2.cloned.1.call-done = bf16[256,6,4,128]{3,2,1,0:T(4,128)(2,1)} async-done(((bf16[8,6,4,128]{3,2,1,0:T(4,128)(2,1)}), bf16[256,6,4,128]{3,2,1,0:T(4,128)(2,1)}) %all-gather.2.cloned.1.call-update) | async-done | bytes 1572880 | tf_op jit(solution)/shard_map/all_gather | solution.py:46
  76.5 3.2 %copy.26 = bf16[256,6,4,1,128]{0,2,4,1,3:T(4,128)(2,1)S(1)} copy(bf16[256,6,4,1,128]{4,2,1,0,3:T(4,128)(2,1)} %bitcast.17) | data formatting | bytes 3145728
  79.8 0.6 pad.clone
  80.4 0.0 copy-start.1
  80.4 0.2 copy.21
  80.7 0.0 copy-done
  80.7 0.4 copy-done.1
  81.1 8.4 %fusion.8 = f32[4,4,8,17,16]{4,2,3,1,0:T(8,128)S(1)} fusion(bf16[16,3,3,3,256]{4,0,3,2,1:T(8,128)(2,1)S(1)} %copy-done, bf16[256,6,4,1,7,2]{0,4,5,2,1,3:T(8,128)(2,1)S(1)} %slice.10, bf16[256,6,4,1,8,17]{0,4,5,2,1,3:T(8,128)(2,1)S(1)} %copy.21, pred[8,17]{0,1:T(8,128)(4,1)S(1)} %copy-done.1), kind=kOutput, calls=%fused_computation.9 | convolution fusion | flops 406718464 | bytes 2203784 | tf_op jit(solution)/shard_map/conv_general_dilated | solution.py:23
  89.5 0.8 copy.22
  90.3 0.3 reshape.9
  90.7 0.3 copy.23
  91.0 1.2 %fusion.11 = bf16[16,2,2,64]{0,3,2,1:T(8,128)(2,1)S(1)} fusion(f32[16,2,2,2,2,64,2]{0,6,5,4,3,2,1:T(2,128)S(1)} %bitcast.16, f32[16]{0:T(128)S(1)} %convert_element_type.6), kind=kLoop, calls=%fused_computation.10 | loop fusion | flops 159744 | bytes 139328 | tf_op jit(solution)/shard_map/reduce_max | solution.py:38
  92.2 0.1 copy.24
  92.3 0.6 copy.25
  (2 shorter events, 0.1 us)
Async XLA Ops:
  6.5 74.2 %copy-start = (bf16[16,3,3,3,256]{4,0,3,2,1:T(8,128)(2,1)S(1)}, bf16[16,3,3,3,256]{4,0,3,2,1:T(8,128)(2,1)}, u32[]{:S(2)}) copy-start(bf16[16,3,3,3,256]{4,0,3,2,1:T(8,128)(2,1)} %param.4) | copy-start | bytes 663556
  6.5 70.0 %all-gather.2.cloned.1.call-start = ((), (), s32[]{:S(2)}) async-start(), calls=%async_computation | async-start | bytes 1622016 | tf_op jit(solution)/shard_map/all_gather | solution.py:46
  7.3 5.2 %collective-permute-start = (bf16[8,1,4,128]{3,2,1,0:T(4,128)(2,1)S(1)}, bf16[8,1,4,128]{3,2,1,0:T(4,128)(2,1)S(1)}, u32[]{:S(2)}, u32[]{:S(2)}) collective-permute-start(bf16[8,1,4,128]{3,2,1,0:T(4,128)(2,1)S(1)} %get-tuple-element.5), channel_id=1, source_target_pairs={{0,1},{1,2},{2,3},{3,4},{4,5},{5,6},{6,7},{8,9},{9,10},{10,11},{11... | collective-permute-start | bytes 24584 | tf_op jit(solution)/shard_map/ppermute | solution.py:14
  11.2 4.4 %collective-permute-start.1 = (bf16[8,1,4,128]{3,2,1,0:T(4,128)(2,1)S(1)}, bf16[8,1,4,128]{3,2,1,0:T(4,128)(2,1)S(1)}, u32[]{:S(2)}, u32[]{:S(2)}) collective-permute-start(bf16[8,1,4,128]{3,2,1,0:T(4,128)(2,1)S(1)} %get-tuple-element.6), channel_id=1, source_target_pairs={{1,0},{2,1},{3,2},{4,3},{5,4},{6,5},{7,6},{9,8},{10,9},{11,10},{12... | collective-permute-start | bytes 24584 | tf_op jit(solution)/shard_map/ppermute | solution.py:17
  80.4 0.7 copy-start.1
Sparse Core Ops, SparseCore 0:
  17.2 59.2 all-gather.1
where the time goes:
time: 100 us; the launch traced here: 99.7 us
  waiting for transfers between devices  61.9 us (62%)
  between operations  13.5 us (14%)
  matrix products  8.37 us (8%)
  local copies, waits for them, and re-layouts  7.48 us (7%)
  starting transfers between devices  5.23 us (5%)
  other arithmetic  3.25 us (3%)
    all_gather x1, waiting for transfers between devices, on_device(): lax.all_gather(padded, 'filt', axis=0, tiled=True)  58.8 us
    conv_general_dilated x1, matrix products, convolve(): lax.conv_general_dilated(inputs[None], weights, (1, 1, 1), padding, dimen...  8.37 us
    ppermute x1, starting transfers between devices, with_halo(): lax.ppermute(lax.slice_in_dim(block, block.shape[dim] - width, None, axis...  3.94 us
    unnamed x5, local copies, waits for them, and re-layouts  3.63 us
    ppermute x1, waiting for transfers between devices, with_halo(): lax.ppermute(lax.slice_in_dim(block, 0, width, axis=dim), axis, backward)  3.08 us
  transfers between devices with their start and end apart: 3, of which 2 were waited for; matrix products, arithmetic and copies ran while one was open for 1% of the time, Pallas kernels for 0%

commit v1 on v0

--- a/solution.py
+++ b/solution.py
@@ -43,7 +43,11 @@
     padded = with_halo(volume, (("space", 1),), 1)
     zeroed = jnp.zeros((kernel.shape[0], slab_depth, height, across), jnp.float32)
     summed = zeroed + convolve(
-        lax.all_gather(padded, "filt", axis=0, tiled=True), kernel, ((0, 0), (1, 1), (1, 1))
+        jnp.concatenate(
+            lax.all_to_all(jnp.stack([padded] * lax.axis_size("filt")), "filt", 0, 0), axis=0
+        ),
+        kernel,
+        ((0, 0), (1, 1), (1, 1)),
     )
     return finish(summed, filter_bias)
 

time: 100 us -> 80 us (0.80)
  the two profiles are of different devices: /device:TPU:1 before, /device:TPU:2 now
where the time goes in v1:
time: 80 us; the launch traced here: 79.7 us
  waiting for transfers between devices  44.5 us (56%)
  starting transfers between devices  17.4 us (22%)
  matrix products  8.38 us (10%)
  local copies, waits for them, and re-layouts  7.26 us (9%)
  other arithmetic  1.98 us (2%)
    all_to_all x1, waiting for transfers between devices, on_device(): lax.all_to_all(jnp.stack([padded] * lax.axis_size('filt')), 'filt', 0, 0)  41.4 us
    all_to_all x1, starting transfers between devices, on_device(): lax.all_to_all(jnp.stack([padded] * lax.axis_size('filt')), 'filt', 0, 0)  11.6 us
    conv_general_dilated x1, matrix products, convolve(): lax.conv_general_dilated(inputs[None], weights, (1, 1, 1), padding, dimen...  8.38 us
    ppermute x1, starting transfers between devices, with_halo(): lax.ppermute(lax.slice_in_dim(block, block.shape[dim] - width, None, axis...  3.39 us
    ppermute x1, waiting for transfers between devices, with_halo(): lax.ppermute(lax.slice_in_dim(block, 0, width, axis=dim), axis, backward)  3.09 us
    ppermute x1, starting transfers between devices, with_halo(): lax.ppermute(lax.slice_in_dim(block, 0, width, axis=dim), axis, backward)  2.44 us
    conv_general_dilated x6, local copies, waits for them, and re-layouts, convolve(): lax.conv_general_dilated(inputs[None], weights, (1, 1, 1), padding, dimen...  1.75 us
  transfers between devices with their start and end apart: 3, of which 2 were waited for; matrix products, arithmetic and copies ran while one was open for 0% of the time, Pallas kernels for 0%

profile of v1, /device:TPU:2, one launch (start us, length us, event | category | flops | bytes accessed | tf_op | source)
XLA Modules:
  0.0 79.7 jit_solution(10329640561818853407)
XLA Ops:
  0.0 0.0 copy-start
  0.0 0.8 fusion.16
  0.8 3.4 %collective-permute-start = (bf16[8,1,4,128]{3,2,1,0:T(4,128)(2,1)S(1)}, bf16[8,1,4,128]{3,2,1,0:T(4,128)(2,1)S(1)}, u32[]{:S(2)}, u32[]{:S(2)}) collective-permute-start(bf16[8,1,4,128]{3,2,1,0:T(4,128)(2,1)S(1)} %get-tuple-element.5), channel_id=1, source_target_pairs={{0,1},{1,2},{2,3},{3,4},{4,5},{5,6},{6,7},{8,9},{9,10},{10,11},{11... | collective-permute-start | bytes 24584 | tf_op jit(solution)/shard_map/ppermute | solution.py:14
  4.2 2.4 %collective-permute-start.1 = (bf16[8,1,4,128]{3,2,1,0:T(4,128)(2,1)S(1)}, bf16[8,1,4,128]{3,2,1,0:T(4,128)(2,1)S(1)}, u32[]{:S(2)}, u32[]{:S(2)}) collective-permute-start(bf16[8,1,4,128]{3,2,1,0:T(4,128)(2,1)S(1)} %get-tuple-element.6), channel_id=1, source_target_pairs={{1,0},{2,1},{3,2},{4,3},{5,4},{6,5},{7,6},{9,8},{10,9},{11,10},{12... | collective-permute-start | bytes 24584 | tf_op jit(solution)/shard_map/ppermute | solution.py:17
  6.6 0.0 collective-permute-done
  6.6 3.1 %collective-permute-done.1 = bf16[8,1,4,128]{3,2,1,0:T(4,128)(2,1)S(1)} collective-permute-done((bf16[8,1,4,128]{3,2,1,0:T(4,128)(2,1)S(1)}, bf16[8,1,4,128]{3,2,1,0:T(4,128)(2,1)S(1)}, u32[]{:S(2)}, u32[]{:S(2)}) %collective-permute-start.1) | collective-permute-done | bytes 8224 | tf_op jit(solution)/shard_map/ppermute | solution.py:17
  9.7 0.8 %pad_maximum_fusion = bf16[8,6,4,128]{3,2,1,0:T(4,128)(2,1)S(1)} fusion(bf16[8,1,4,128]{3,2,1,0:T(4,128)(2,1)S(1)} %collective-permute-done.1, bf16[8,4,4,128]{3,2,1,0:T(4,128)(2,1)} %param.3, bf16[8,1,4,128]{3,2,1,0:T(4,128)(2,1)S(1)} %collective-permute-done), kind=kLoop, calls=%fused_computation.14 | loop fusion | flops 49152 | bytes 98304 | tf_op jit(solution)/shard_map/concatenate | solution.py:18
  10.5 1.5 %stack.2 = bf16[32,8,6,4,128]{4,1,3,2,0:T(8,128)(2,1)} broadcast(bf16[8,6,4,128]{3,0,2,1:T(8,128)(2,1)S(1)} %copy.22), dimensions={1,2,3,4} | broadcast | bytes 1622016 | tf_op jit(solution)/shard_map/stack | solution.py:47
  12.0 11.6 %all-to-all-start = ((bf16[32,8,6,4,128]{4,1,3,2,0:T(8,128)(2,1)}), bf16[32,8,6,4,128]{4,1,3,2,0:T(8,128)(2,1)S(1)}, u32[]{:S(2)}, u32[]{:S(2)}) async-start(bf16[32,8,6,4,128]{4,1,3,2,0:T(8,128)(2,1)} %stack.2), calls=%async_computation | async-start | bytes 3145728 | tf_op jit(solution)/shard_map/all_to_all | solution.py:47
  23.7 0.0 copy-done.1
  23.7 41.4 %all-to-all-done = bf16[32,8,6,4,128]{4,1,3,2,0:T(8,128)(2,1)S(1)} async-done(((bf16[32,8,6,4,128]{4,1,3,2,0:T(8,128)(2,1)}), bf16[32,8,6,4,128]{4,1,3,2,0:T(8,128)(2,1)S(1)}, u32[]{:S(2)}, u32[]{:S(2)}) %all-to-all-start) | async-done | bytes 1572896 | tf_op jit(solution)/shard_map/all_to_all | solution.py:47
  65.1 0.4 copy.33
  65.5 1.1 %copy.31 = bf16[256,6,4,1,128]{0,2,4,1,3:T(4,128)(2,1)S(1)} copy(bf16[256,6,4,1,128]{4,0,2,1,3:T(8,128)(2,1)S(1)} %bitcast.18) | data formatting | bytes 3145728
  66.6 0.6 pad.clone
  67.2 0.0 copy-start.2
  67.2 0.2 copy.26
  67.5 0.4 copy-done.2
  67.9 8.4 %fusion.8 = f32[4,4,8,17,16]{4,2,3,1,0:T(8,128)S(1)} fusion(bf16[16,3,3,3,256]{4,0,3,2,1:T(8,128)(2,1)S(1)} %copy-done, bf16[256,6,4,1,7,2]{0,4,5,2,1,3:T(8,128)(2,1)S(1)} %slice.10, bf16[256,6,4,1,8,17]{0,4,5,2,1,3:T(8,128)(2,1)S(1)} %copy.26, pred[8,17]{0,1:T(8,128)(4,1)S(1)} %copy-done.2), kind=kOutput, calls=%fused_computation.10 | convolution fusion | flops 406718464 | bytes 2203784 | tf_op jit(solution)/shard_map/conv_general_dilated | solution.py:23
  76.3 0.8 %copy.27 = f32[4,4,8,17,16]{3,2,4,1,0:T(8,128)S(1)} copy(f32[4,4,8,17,16]{4,2,3,1,0:T(8,128)S(1)} %fusion.8) | data formatting | bytes 278528 | tf_op jit(solution)/shard_map/conv_general_dilated | solution.py:23
  77.1 0.3 reshape.11
  77.5 0.3 copy.28
  77.8 1.2 %fusion.11 = bf16[16,2,2,64]{0,3,2,1:T(8,128)(2,1)S(1)} fusion(f32[16,2,2,2,2,64,2]{0,6,5,4,3,2,1:T(2,128)S(1)} %bitcast.19, f32[16]{0:T(128)S(1)} %convert_element_type.6), kind=kLoop, calls=%fused_computation.11 | loop fusion | flops 159744 | bytes 139328 | tf_op jit(solution)/shard_map/reduce_max | solution.py:38
  79.0 0.1 copy.29
  79.1 0.6 copy.30
  (6 shorter events, 0.1 us)
Async XLA Ops:
  0.0 67.5 %copy-start = (bf16[16,3,3,3,256]{4,0,3,2,1:T(8,128)(2,1)S(1)}, bf16[16,3,3,3,256]{4,0,3,2,1:T(8,128)(2,1)}, u32[]{:S(2)}) copy-start(bf16[16,3,3,3,256]{4,0,3,2,1:T(8,128)(2,1)} %param.4) | copy-start | bytes 663556
  0.8 5.8 %collective-permute-start = (bf16[8,1,4,128]{3,2,1,0:T(4,128)(2,1)S(1)}, bf16[8,1,4,128]{3,2,1,0:T(4,128)(2,1)S(1)}, u32[]{:S(2)}, u32[]{:S(2)}) collective-permute-start(bf16[8,1,4,128]{3,2,1,0:T(4,128)(2,1)S(1)} %get-tuple-element.5), channel_id=1, source_target_pairs={{0,1},{1,2},{2,3},{3,4},{4,5},{5,6},{6,7},{8,9},{9,10},{10,11},{11... | collective-permute-start | bytes 24584 | tf_op jit(solution)/shard_map/ppermute | solution.py:14
  4.2 5.5 %collective-permute-start.1 = (bf16[8,1,4,128]{3,2,1,0:T(4,128)(2,1)S(1)}, bf16[8,1,4,128]{3,2,1,0:T(4,128)(2,1)S(1)}, u32[]{:S(2)}, u32[]{:S(2)}) collective-permute-start(bf16[8,1,4,128]{3,2,1,0:T(4,128)(2,1)S(1)} %get-tuple-element.6), channel_id=1, source_target_pairs={{1,0},{2,1},{3,2},{4,3},{5,4},{6,5},{7,6},{9,8},{10,9},{11,10},{12... | collective-permute-start | bytes 24584 | tf_op jit(solution)/shard_map/ppermute | solution.py:17
  12.0 11.6 %copy-start.1 = (bf16[16]{0:T(256)(128)(2,1)S(1)}, bf16[16]{0:T(256)(128)(2,1)}, u32[]{:S(2)}) copy-start(bf16[16]{0:T(256)(128)(2,1)} %param.5) | copy-start | bytes 100
  12.0 53.0 %all-to-all-start = ((bf16[32,8,6,4,128]{4,1,3,2,0:T(8,128)(2,1)}), bf16[32,8,6,4,128]{4,1,3,2,0:T(8,128)(2,1)S(1)}, u32[]{:S(2)}, u32[]{:S(2)}) async-start(bf16[32,8,6,4,128]{4,1,3,2,0:T(8,128)(2,1)} %stack.2), calls=%async_computation | async-start | bytes 3145728 | tf_op jit(solution)/shard_map/all_to_all | solution.py:47
  67.2 0.7 copy-start.2
